TPU v7x, 32 devices: a whole 2x2x4 slice. The times are simulated.
32 devices in a mesh: gx: 4 (over z), gy: 4 (over x, core), gz: 2 (over y).
Axes of the slice: x: 2, y: 2, z: 4, core: 2. Of those that a mesh axis runs over, the one named last changes fastest.
Arguments:
- activations: bfloat16 [1024, 8192], P('gy', 'gx'), may hold values from -0.5 to 0.5
- cotangent: bfloat16 [1024, 8192], P('gy', 'gx'), may hold values from -1.5 to 1.5
- gate_pre: bfloat16 [1024, 26624], P('gx', ('gy', 'gz')), may hold values from -6 to 6
- up_pre: bfloat16 [1024, 26624], P('gx', ('gy', 'gz')), may hold values from -6 to 6
- gate_weight: bfloat16 [8192, 26624], P('gx', ('gy', 'gz')), may hold values from -0.0625 to 0.0625
- up_weight: bfloat16 [8192, 26624], P('gx', ('gy', 'gz')), may hold values from -0.0625 to 0.0625
- down_weight: bfloat16 [26624, 8192], P(('gy', 'gz'), 'gx'), may hold values from -0.15625 to 0.15625
Outputs:
- input_grad: bfloat16 [1024, 8192], P('gy', 'gx')
- gate_grad: bfloat16 [8192, 26624], P('gx', ('gy', 'gz'))
- up_grad: bfloat16 [8192, 26624], P('gx', ('gy', 'gz'))
- down_grad: bfloat16 [26624, 8192], P(('gy', 'gz'), 'gx')
All inputs are finite; a program needn't handle non-finite values.
Results may differ from a plain program's by a relative error of at most 0.015.
Values may be sent and summed in bfloat16 or wider, within the bound.
A program may use at most 192 MiB of HBM per device.

v0:
```python
import jax
import jax.numpy as jnp
from jax import lax
from jax.sharding import PartitionSpec as P

over_rows = (((0,), (0,)), ((), ()))
over_cols = (((1,), (1,)), ((), ()))


def swiglu_grads(gate_in, up_in, grad_hidden):
    gate_val = gate_in.astype(jnp.float32)
    up_val = up_in.astype(jnp.float32)
    sigmoid = jax.nn.sigmoid(gate_val)
    hidden = (gate_val * sigmoid * up_val).astype(jnp.bfloat16)
    grad_gate = (grad_hidden * up_val * sigmoid * (1.0 + gate_val * (1.0 - sigmoid))).astype(
        jnp.bfloat16
    )
    grad_up = (grad_hidden * gate_val * sigmoid).astype(jnp.bfloat16)
    return (hidden, grad_gate, grad_up)


def input_terms(grad_gate, grad_up, gate_weight, up_weight):

    def compute(offset, amount):
        total = lax.dot_general(
            grad_gate, gate_weight, over_cols, preferred_element_type=jnp.float32
        )
        return total + lax.dot_general(
            grad_up, up_weight, over_cols, preferred_element_type=jnp.float32
        )

    return compute


def shards(activations, cotangent, gate_pre, up_pre, gate_weight, up_weight, down_weight):
    cotangent_all = lax.all_gather(cotangent, "gy", axis=0, tiled=True)
    gate_all, up_all = (
        lax.all_gather(gate_pre, "gx", axis=0, tiled=True),
        lax.all_gather(up_pre, "gx", axis=0, tiled=True),
    )
    local_sum = lax.dot_general(
        cotangent_all, down_weight, over_cols, preferred_element_type=jnp.float32
    )
    grad_hidden = lax.psum(local_sum, "gx")
    hidden, grad_gate, grad_up = swiglu_grads(gate_all, up_all, grad_hidden)
    down_grad = lax.dot_general(
        hidden, cotangent_all, over_rows, preferred_element_type=jnp.float32
    ).astype(jnp.bfloat16)
    segment = lax.all_gather(activations, "gy", axis=0, tiled=True)
    first = lax.dot_general(segment, grad_gate, over_rows, preferred_element_type=jnp.float32)
    second = lax.dot_general(segment, grad_up, over_rows, preferred_element_type=jnp.float32)
    row_count = activations.shape[0]
    terms = input_terms(grad_gate, grad_up, gate_weight, up_weight)
    share_rows = row_count // lax.axis_size("gz")
    input_share = lax.psum_scatter(
        terms(jnp.int32(0), lax.axis_size(("gy", "gz")) * share_rows),
        ("gy", "gz"),
        scatter_dimension=0,
        tiled=True,
    )
    input_grad = lax.all_gather(input_share.astype(jnp.bfloat16), "gz", axis=0, tiled=True)
    return (input_grad, first.astype(jnp.bfloat16), second.astype(jnp.bfloat16), down_grad)


def solution(mesh):
    in_specs = (
        P("gy", "gx"),
        P("gy", "gx"),
        P("gx", ("gy", "gz")),
        P("gx", ("gy", "gz")),
        P("gx", ("gy", "gz")),
        P("gx", ("gy", "gz")),
        P(("gy", "gz"), "gx"),
    )
    out_specs = (P("gy", "gx"), P("gx", ("gy", "gz")), P("gx", ("gy", "gz")), P(("gy", "gz"), "gx"))
    return jax.shard_map(shards, mesh=mesh, in_specs=in_specs, out_specs=out_specs, check_vma=False)
```

profile of v0, /device:TPU:0, one launch (start us, length us, event | category | flops | bytes accessed | tf_op | source)
XLA Modules:
  0.0 951.3 jit_solution(15693381875679629747)
XLA Ops:
  7.2 0.0 all-gather.6.cloned.1.call-start
  7.2 0.7 all-gather.6.cloned.1.call-update
  7.9 0.0 all-gather.10.cloned.1.call-start
  7.9 0.7 all-gather.10.cloned.1.call-update
  8.6 0.0 all-gather.8.cloned.1.call-start
  8.7 0.7 all-gather.8.cloned.1.call-update
  9.4 0.0 all-reduce.2.cloned.1.call-start
  9.4 37.3 %all-gather.6.cloned.1.call-done = bf16[1024,2048]{1,0:T(8,128)(2,1)} async-done(((bf16[256,2048]{1,0:T(8,128)(2,1)}), bf16[1024,2048]{1,0:T(8,128)(2,1)}) %all-gather.6.cloned.1.call-update) | async-done | bytes 4194320 | tf_op jit(solution)/shard_map/all_gather | solution.py:36
  46.8 22.5 %fusion.17 = f32[1024,3328]{1,0:T(8,128)} fusion(bf16[1024,2048]{1,0:T(8,128)(2,1)} %all-gather.6.cloned.1.call-done, bf16[3328,2048]{1,0:T(8,128)(2,1)} %param.13), kind=kOutput, calls=%fused_computation.24 | convolution fusion | flops 13958643712 | bytes 31457280 | tf_op jit(solution)/shard_map/dot_general | solution.py:41
  69.3 0.0 all-reduce.2.cloned.1.call-update
  69.3 0.0 all-gather.14.cloned.1.call-start
  69.4 0.5 all-gather.14.cloned.1.call-update
  69.9 0.2 reduce-scatter.2.cloned.1.call-start
  70.2 102.1 %all-gather.10.cloned.1.call-done = bf16[1024,3328]{1,0:T(8,128)(2,1)} async-done(((bf16[256,3328]{1,0:T(8,128)(2,1)}), bf16[1024,3328]{1,0:T(8,128)(2,1)}) %all-gather.10.cloned.1.call-update) | async-done | bytes 6815760 | tf_op jit(solution)/shard_map/all_gather | solution.py:38
  172.3 123.8 %all-gather.8.cloned.1.call-done = bf16[1024,3328]{1,0:T(8,128)(2,1)} async-done(((bf16[256,3328]{1,0:T(8,128)(2,1)}), bf16[1024,3328]{1,0:T(8,128)(2,1)}) %all-gather.8.cloned.1.call-update) | async-done | bytes 6815760 | tf_op jit(solution)/shard_map/all_gather | solution.py:39
  296.1 461.1 %all-reduce.2.cloned.1.call-done = f32[1024,3328]{1,0:T(8,128)} async-done(((f32[1024,3328]{1,0:T(8,128)}), f32[1024,3328]{1,0:T(8,128)}) %all-reduce.2.cloned.1.call-update) | async-done | bytes 13631504 | tf_op jit(solution)/shard_map/psum | solution.py:44
  757.1 12.2 %fusion.2 = bf16[1024,3328]{1,0:T(8,128)(2,1)S(1)} fusion(f32[1024,3328]{1,0:T(8,128)} %all-reduce.2.cloned.1.call-done, bf16[1024,3328]{1,0:T(8,128)(2,1)} %all-gather.8.cloned.1.call-done, bf16[1024,3328]{1,0:T(8,128)(2,1)} %all-gather.10.cloned.1.call-done), kind=kLoop, calls=%fused_computation.11 | loop fusion | flops 40894464 | bytes 34078720 | tf_op jit(solution)/shard_map/convert_element_type | solution.py:15
  769.3 0.0 copy-start
  769.3 2.9 copy-done
  772.2 18.1 %fusion.18 = f32[1024,2048]{1,0:T(8,128)} fusion(bf16[1024,3328]{1,0:T(8,128)(2,1)S(1)} %fusion.2, bf16[2048,3328]{1,0:T(8,128)(2,1)} %param.11), kind=kOutput, calls=%fused_computation.25 | convolution fusion | flops 13958643712 | bytes 28835840 | tf_op jit(solution)/shard_map/dot_general | solution.py:25
  790.3 24.1 %convolution_add_fusion = f32[1024,2048]{1,0:T(8,128)} fusion(f32[1024,2048]{1,0:T(8,128)} %fusion.18, bf16[2048,3328]{1,0:T(8,128)(2,1)} %param.12, f32[1024,3328]{1,0:T(8,128)} %all-reduce.2.cloned.1.call-done, bf16[1024,3328]{1,0:T(8,128)(2,1)} %all-gather.10.cloned.1.call-done), kind=kOutput, calls=%fused_computation.22 | convolution fusion | flops 13984595968 | bytes 50855936 | tf_op jit(solution)/shard_map/dot_general | solution.py:28
  814.4 0.0 reduce-scatter.2.cloned.1.call-update
  814.4 0.3 all-gather.12.cloned.1.call-start
  814.7 23.9 %convolution_convert_fusion = bf16[3328,2048]{1,0:T(8,128)(2,1)} fusion(bf16[1024,2048]{1,0:T(8,128)(2,1)} %all-gather.6.cloned.1.call-done, bf16[1024,3328]{1,0:T(8,128)(2,1)} %all-gather.8.cloned.1.call-done, bf16[1024,3328]{1,0:T(8,128)(2,1)} %all-gather.10.cloned.1.call-done), kind=kOutput, calls=%fused_computation.6 | convolution fusion | flops 13992722432 | bytes 31457280 | tf_op jit(solution)/shard_map/dot_general | solution.py:46
  838.6 0.0 all-gather.14.cloned.1.call-done
  838.6 23.5 %fusion.11 = bf16[2048,3328]{0,1:T(8,128)(2,1)} fusion(bf16[1024,2048]{1,0:T(8,128)(2,1)} %all-gather.14.cloned.1.call-done, f32[1024,3328]{1,0:T(8,128)} %all-reduce.2.cloned.1.call-done, bf16[1024,3328]{1,0:T(8,128)(2,1)} %all-gather.10.cloned.1.call-done), kind=kOutput, calls=%fused_computation.20 | convolution fusion | flops 13989314560 | bytes 38273024 | tf_op jit(solution)/shard_map/dot_general | solution.py:51
  862.1 22.0 %reduce-scatter.2.cloned.1.call-done = f32[128,2048]{1,0:T(8,128)} async-done(((f32[1024,2048]{1,0:T(8,128)}), f32[128,2048]{1,0:T(8,128)}) %reduce-scatter.2.cloned.1.call-update) | async-done | bytes 1048592 | tf_op jit(solution)/shard_map/reduce_scatter | solution.py:55
  884.1 2.1 convert_element_type.37
  886.2 0.0 all-gather.12.cloned.1.call-update
  886.2 21.0 %fusion.10 = bf16[2048,3328]{0,1:T(8,128)(2,1)} fusion(bf16[1024,3328]{1,0:T(8,128)(2,1)} %copy-done, bf16[1024,2048]{1,0:T(8,128)(2,1)} %all-gather.14.cloned.1.call-done), kind=kOutput, calls=%fused_computation.19 | convolution fusion | flops 13965459456 | bytes 24641536 | tf_op jit(solution)/shard_map/dot_general | solution.py:50
  907.3 17.4 %copy.11 = bf16[2048,3328]{1,0:T(8,128)(2,1)} copy(bf16[2048,3328]{0,1:T(8,128)(2,1)} %fusion.10) | data formatting | bytes 27262976
  924.7 17.4 %copy.12 = bf16[2048,3328]{1,0:T(8,128)(2,1)} copy(bf16[2048,3328]{0,1:T(8,128)(2,1)} %fusion.11) | data formatting | bytes 27262976
  942.1 0.0 all-gather.12.cloned.1.call-done
  942.2 2.3 copy.15
Async XLA Ops:
  7.2 39.6 %all-gather.6.cloned.1.call-start = ((), (), s32[]{:S(2)}) async-start(), calls=%async_computation.1 | async-start | bytes 5242880 | tf_op jit(solution)/shard_map/all_gather | solution.py:36
  7.9 164.4 %all-gather.10.cloned.1.call-start = ((), (), s32[]{:S(2)}) async-start(), calls=%async_computation.4 | async-start | bytes 8519680 | tf_op jit(solution)/shard_map/all_gather | solution.py:38
  8.6 287.4 %all-gather.8.cloned.1.call-start = ((), (), s32[]{:S(2)}) async-start(), calls=%async_computation.3 | async-start | bytes 8519680 | tf_op jit(solution)/shard_map/all_gather | solution.py:39
  9.4 747.8 %all-reduce.2.cloned.1.call-start = ((), (), s32[]{:S(2)}) async-start(), calls=%async_computation.2 | async-start | bytes 27262976 | tf_op jit(solution)/shard_map/psum | solution.py:44
  69.3 769.3 %all-gather.14.cloned.1.call-start = ((), (), s32[]{:S(2)}) async-start(), calls=%async_computation.7 | async-start | bytes 5242880 | tf_op jit(solution)/shard_map/all_gather | solution.py:49
  69.9 814.2 %reduce-scatter.2.cloned.1.call-start = ((), (), s32[]{:S(2)}) async-start(), calls=%async_computation.5 | async-start | bytes 9437184 | tf_op jit(solution)/shard_map/reduce_scatter | solution.py:55
  769.3 2.9 copy-start
  814.4 127.7 %all-gather.12.cloned.1.call-start = ((), (), s32[]{:S(2)}) async-start(), calls=%async_computation.6 | async-start | bytes 1572864 | tf_op jit(solution)/shard_map/all_gather | solution.py:61
Sparse Core Ops, SparseCore 0:
  9.6 37.1 all-gather.5
  48.3 123.9 all-gather.9
  173.9 122.1 all-gather.7
  299.0 458.1 all-reduce.1
  758.6 33.3 all-gather.13
  814.6 69.5 reduce-scatter.1
  886.4 21.2 all-gather.11
where the time goes:
time: 952 us; the launch traced here: 951 us
  waiting for transfers between devices  749 us (79%)
  matrix products  133 us (14%)
  local copies, waits for them, and re-layouts  40.1 us (4%)
  other arithmetic  14.3 us (2%)
  between operations  14.1 us (1%)
    psum x1, waiting for transfers between devices, shards(): grad_hidden = lax.psum(local_sum, 'gx')  461 us
    all_gather x1, waiting for transfers between devices, shards(): lax.all_gather(up_pre, 'gx', axis=0, tiled=True)  124 us
    all_gather x1, waiting for transfers between devices, shards(): lax.all_gather(gate_pre, 'gx', axis=0, tiled=True)  102 us
    unnamed x5, local copies, waits for them, and re-layouts  40.1 us
    all_gather x1, waiting for transfers between devices, shards(): cotangent_all = lax.all_gather(cotangent, 'gy', axis=0, tiled=True)  37.3 us
    dot_general x1, matrix products, compute(): lax.dot_general(grad_up, up_weight, over_cols, preferred_element_type=jnp...  24.1 us
    dot_general x1, matrix products, shards(): lax.dot_general(hidden, cotangent_all, over_rows, preferred_element_type=...  23.9 us
    dot_general x1, matrix products, shards(): lax.dot_general(segment, grad_up, over_rows, preferred_element_type=jnp.f...  23.5 us
  transfers between devices with their start and end apart: 7, of which 5 were waited for; matrix products, arithmetic and copies ran while one was open for 19% of the time, Pallas kernels for 0%

commit v1 on v0

--- a/solution.py
+++ b/solution.py
@@ -5,6 +5,15 @@
 
 over_rows = (((0,), (0,)), ((), ()))
 over_cols = (((1,), (1,)), ((), ()))
+
+
+def doubling_sum(x, name):
+    size = lax.axis_size(name)
+    total, far = (x, 1)
+    while far < size:
+        total = total + lax.ppermute(total, name, [(i, i ^ far) for i in range(size)])
+        far = 2 * far
+    return total
 
 
 def swiglu_grads(gate_in, up_in, grad_hidden):
@@ -41,7 +50,7 @@
     local_sum = lax.dot_general(
         cotangent_all, down_weight, over_cols, preferred_element_type=jnp.float32
     )
-    grad_hidden = lax.psum(local_sum, "gx")
+    grad_hidden = doubling_sum(local_sum, "gx")
     hidden, grad_gate, grad_up = swiglu_grads(gate_all, up_all, grad_hidden)
     down_grad = lax.dot_general(
         hidden, cotangent_all, over_rows, preferred_element_type=jnp.float32

time: 952 us -> 1390 us (1.46)
  waiting for transfers between devices: 749 us -> 1160 us
  other arithmetic: 14.3 us -> 34.1 us
    ppermute x0 -> x2, waiting for transfers between devices: none -> 639 us  [doubling_sum(): lax.ppermute(total, name, [(i, i ^ far) for i in range(size)])]
    psum x1 -> x0, waiting for transfers between devices: 461 us -> none  [shards(): grad_hidden = lax.psum(local_sum, 'gx')]
    all_gather x1, waiting for transfers between devices: 124 us -> 458 us  [shards(): lax.all_gather(up_pre, 'gx', axis=0, tiled=True)]
    all_gather x1, waiting for transfers between devices: 102 us -> 0.03 us  [shards(): lax.all_gather(gate_pre, 'gx', axis=0, tiled=True)]
    add x0 -> x1, other arithmetic: none -> 14.9 us  [doubling_sum(): total + lax.ppermute(total, name, [(i, i ^ far) for i in range(size)])]
  transfers between devices with their start and end apart: 7 -> 8, of which waited for: 5 -> 5; matrix products, arithmetic and copies ran while one was open for 19% -> 13% of each run, Pallas kernels for 0% -> 0%
where the time goes in v1:
time: 1390 us
  waiting for transfers between devices  1160 us (83%)
  matrix products  132 us (9%)
  local copies, waits for them, and re-layouts  37.2 us (3%)
  other arithmetic  34.1 us (2%)
  between operations  15.7 us (1%)
    ppermute x2, waiting for transfers between devices, doubling_sum(): lax.ppermute(total, name, [(i, i ^ far) for i in range(size)])  639 us
    all_gather x1, waiting for transfers between devices, shards(): lax.all_gather(up_pre, 'gx', axis=0, tiled=True)  458 us
    all_gather x1, waiting for transfers between devices, shards(): cotangent_all = lax.all_gather(cotangent, 'gy', axis=0, tiled=True)  38.8 us
    unnamed x5, local copies, waits for them, and re-layouts  37.2 us
  transfers between devices with their start and end apart: 8, of which 5 were waited for; matrix products, arithmetic and copies ran while one was open for 13% of the time, Pallas kernels for 0%

profile of v1, /device:TPU:0, one launch (start us, length us, event | category | flops | bytes accessed | tf_op | source)
XLA Modules:
  0.0 1386.5 jit_solution(9120587338531507366)
XLA Ops:
  8.0 0.0 all-gather.6.cloned.1.call-start
  8.0 0.7 all-gather.6.cloned.1.call-update
  8.7 0.0 all-gather.10.cloned.1.call-start
  8.8 38.8 %all-gather.6.cloned.1.call-done = bf16[1024,2048]{1,0:T(8,128)(2,1)} async-done(((bf16[256,2048]{1,0:T(8,128)(2,1)}), bf16[1024,2048]{1,0:T(8,128)(2,1)}) %all-gather.6.cloned.1.call-update) | async-done | bytes 4194320 | tf_op jit(solution)/shard_map/all_gather | solution.py:45
  47.6 22.5 %fusion.16 = f32[1024,3328]{1,0:T(8,128)} fusion(bf16[1024,2048]{1,0:T(8,128)(2,1)} %all-gather.6.cloned.1.call-done, bf16[3328,2048]{1,0:T(8,128)(2,1)} %param.13), kind=kOutput, calls=%fused_computation.24 | convolution fusion | flops 13958643712 | bytes 31457280 | tf_op jit(solution)/shard_map/dot_general | solution.py:50
  70.2 1.5 collective-permute-start
  71.6 0.0 all-gather.10.cloned.1.call-update
  71.7 0.0 all-gather.8.cloned.1.call-start
  71.7 403.3 %collective-permute-done = f32[1024,3328]{1,0:T(8,128)} collective-permute-done((f32[1024,3328]{1,0:T(8,128)}, f32[1024,3328]{1,0:T(8,128)}, u32[]{:S(2)}, u32[]{:S(2)}) %collective-permute-start) | collective-permute-done | bytes 13631520 | tf_op jit(solution)/shard_map/ppermute | solution.py:14
  475.0 14.9 %add.17 = f32[1024,3328]{1,0:T(8,128)} add(f32[1024,3328]{1,0:T(8,128)} %fusion.16, f32[1024,3328]{1,0:T(8,128)} %collective-permute-done) | non-fusion elementwise | flops 3407872 | bytes 40894464 | tf_op jit(solution)/shard_map/add | solution.py:14
  489.9 2.4 collective-permute-start.1
  492.3 0.0 all-gather.8.cloned.1.call-update
  492.3 0.0 all-gather.14.cloned.1.call-start
  492.4 0.5 all-gather.14.cloned.1.call-update
  492.9 0.3 reduce-scatter.2.cloned.1.call-start
  493.2 0.0 all-gather.10.cloned.1.call-done
  493.3 457.6 %all-gather.8.cloned.1.call-done = bf16[1024,3328]{1,0:T(8,128)(2,1)} async-done(((bf16[256,3328]{1,0:T(8,128)(2,1)}), bf16[1024,3328]{1,0:T(8,128)(2,1)}) %all-gather.8.cloned.1.call-update) | async-done | bytes 6815760 | tf_op jit(solution)/shard_map/all_gather | solution.py:48
  950.9 236.1 %collective-permute-done.1 = f32[1024,3328]{1,0:T(8,128)} collective-permute-done((f32[1024,3328]{1,0:T(8,128)}, f32[1024,3328]{1,0:T(8,128)}, u32[]{:S(2)}, u32[]{:S(2)}) %collective-permute-start.1) | collective-permute-done | bytes 13631520 | tf_op jit(solution)/shard_map/ppermute | solution.py:14
  1187.0 17.1 %fusion.9 = (bf16[1024,3328]{1,0:T(8,128)(2,1)S(1)}, bf16[1024,3328]{1,0:T(8,128)(2,1)}) fusion(bf16[1024,3328]{1,0:T(8,128)(2,1)} %all-gather.10.cloned.1.call-done, f32[1024,3328]{1,0:T(8,128)} %add.17, f32[1024,3328]{1,0:T(8,128)} %collective-permute-done.1, bf16[1024,3328]{1,0:T(8,128)(2,1)} %all-gather.8.cloned.1.call-done), kind=kLoop, calls=%fused_computation.18 | loop fusion | flops 54525952 | bytes 54525952 | tf_op jit(solution)/shard_map/convert_element_type | solution.py:27
  1204.1 0.0 copy-start
  1204.1 20.6 %fusion.17 = f32[1024,2048]{1,0:T(8,128)} fusion(bf16[1024,3328]{1,0:T(8,128)(2,1)S(1)} %get-tuple-element.8, bf16[2048,3328]{1,0:T(8,128)(2,1)} %param.12), kind=kOutput, calls=%fused_computation.25 | convolution fusion | flops 13958643712 | bytes 28835840 | tf_op jit(solution)/shard_map/dot_general | solution.py:37
  1224.7 0.0 copy-done
  1224.7 22.6 %fusion.15 = f32[1024,2048]{1,0:T(8,128)} fusion(f32[1024,2048]{1,0:T(8,128)} %fusion.17, bf16[1024,3328]{1,0:T(8,128)(2,1)} %get-tuple-element.9, bf16[2048,3328]{1,0:T(8,128)(2,1)} %param.11), kind=kOutput, calls=%fused_computation.23 | convolution fusion | flops 13960740864 | bytes 37224448 | tf_op jit(solution)/shard_map/dot_general | solution.py:34
  1247.3 0.0 reduce-scatter.2.cloned.1.call-update
  1247.3 0.6 all-gather.12.cloned.1.call-start
  1247.9 23.4 %convolution_convert_fusion = bf16[3328,2048]{1,0:T(8,128)(2,1)} fusion(bf16[1024,2048]{1,0:T(8,128)(2,1)} %all-gather.6.cloned.1.call-done, bf16[1024,3328]{1,0:T(8,128)(2,1)} %all-gather.8.cloned.1.call-done, bf16[1024,3328]{1,0:T(8,128)(2,1)} %all-gather.10.cloned.1.call-done), kind=kOutput, calls=%fused_computation.6 | convolution fusion | flops 13992722432 | bytes 31457280 | tf_op jit(solution)/shard_map/dot_general | solution.py:55
  1271.3 0.0 all-gather.14.cloned.1.call-done
  1271.3 21.6 %fusion.10 = bf16[2048,3328]{0,1:T(8,128)(2,1)} fusion(bf16[1024,3328]{1,0:T(8,128)(2,1)} %get-tuple-element.9, bf16[1024,2048]{1,0:T(8,128)(2,1)} %all-gather.14.cloned.1.call-done), kind=kOutput, calls=%fused_computation.19 | convolution fusion | flops 13965459456 | bytes 24641536 | tf_op jit(solution)/shard_map/dot_general | solution.py:59
  1292.9 25.9 %reduce-scatter.2.cloned.1.call-done = f32[128,2048]{1,0:T(8,128)} async-done(((f32[1024,2048]{1,0:T(8,128)}), f32[128,2048]{1,0:T(8,128)}) %reduce-scatter.2.cloned.1.call-update) | async-done | bytes 1048592 | tf_op jit(solution)/shard_map/reduce_scatter | solution.py:64
  1318.7 2.1 convert_element_type.37
  1320.8 0.0 all-gather.12.cloned.1.call-update
  1320.8 20.9 %fusion.11 = bf16[2048,3328]{0,1:T(8,128)(2,1)} fusion(bf16[1024,3328]{1,0:T(8,128)(2,1)} %copy-done, bf16[1024,2048]{1,0:T(8,128)(2,1)} %all-gather.14.cloned.1.call-done), kind=kOutput, calls=%fused_computation.20 | convolution fusion | flops 13965459456 | bytes 24641536 | tf_op jit(solution)/shard_map/dot_general | solution.py:60
  1341.8 17.4 %copy.11 = bf16[2048,3328]{1,0:T(8,128)(2,1)} copy(bf16[2048,3328]{0,1:T(8,128)(2,1)} %fusion.10) | data formatting | bytes 27262976
  1359.2 17.4 %copy.12 = bf16[2048,3328]{1,0:T(8,128)(2,1)} copy(bf16[2048,3328]{0,1:T(8,128)(2,1)} %fusion.11) | data formatting | bytes 27262976
  1376.6 0.0 all-gather.12.cloned.1.call-done
  1376.7 2.3 copy.14
Async XLA Ops:
  8.0 39.6 %all-gather.6.cloned.1.call-start = ((), (), s32[]{:S(2)}) async-start(), calls=%async_computation.1 | async-start | bytes 5242880 | tf_op jit(solution)/shard_map/all_gather | solution.py:45
  8.7 484.5 %all-gather.10.cloned.1.call-start = ((), (), s32[]{:S(2)}) async-start(), calls=%async_computation.3 | async-start | bytes 8519680 | tf_op jit(solution)/shard_map/all_gather | solution.py:47
  70.2 404.8 %collective-permute-start = (f32[1024,3328]{1,0:T(8,128)}, f32[1024,3328]{1,0:T(8,128)}, u32[]{:S(2)}, u32[]{:S(2)}) collective-permute-start(f32[1024,3328]{1,0:T(8,128)} %fusion.16), channel_id=1, source_target_pairs={{0,8},{8,0},{16,24},{24,16},{1,9},{9,1},{17,25},{25,17},{2,10},{10... | collective-permute-start | bytes 40894472 | tf_op jit(solution)/shard_map/ppermute | solution.py:14
  71.7 879.2 %all-gather.8.cloned.1.call-start = ((), (), s32[]{:S(2)}) async-start(), calls=%async_computation.2 | async-start | bytes 8519680 | tf_op jit(solution)/shard_map/all_gather | solution.py:48
  489.9 697.1 %collective-permute-start.1 = (f32[1024,3328]{1,0:T(8,128)}, f32[1024,3328]{1,0:T(8,128)}, u32[]{:S(2)}, u32[]{:S(2)}) collective-permute-start(f32[1024,3328]{1,0:T(8,128)} %add.17), channel_id=1, source_target_pairs={{0,16},{8,24},{16,0},{24,8},{1,17},{9,25},{17,1},{25,9},{2,18},{10... | collective-permute-start | bytes 40894472 | tf_op jit(solution)/shard_map/ppermute | solution.py:14
  492.3 779.0 %all-gather.14.cloned.1.call-start = ((), (), s32[]{:S(2)}) async-start(), calls=%async_computation.6 | async-start | bytes 5242880 | tf_op jit(solution)/shard_map/all_gather | solution.py:58
  492.9 825.8 %reduce-scatter.2.cloned.1.call-start = ((), (), s32[]{:S(2)}) async-start(), calls=%async_computation.4 | async-start | bytes 9437184 | tf_op jit(solution)/shard_map/reduce_scatter | solution.py:64
  1204.1 20.6 %copy-start = (bf16[1024,3328]{1,0:T(8,128)(2,1)}, bf16[1024,3328]{1,0:T(8,128)(2,1)S(1)}, u32[]{:S(2)}) copy-start(bf16[1024,3328]{1,0:T(8,128)(2,1)S(1)} %get-tuple-element.8) | copy-start | bytes 20447236
  1247.3 129.3 %all-gather.12.cloned.1.call-start = ((), (), s32[]{:S(2)}) async-start(), calls=%async_computation.5 | async-start | bytes 1572864 | tf_op jit(solution)/shard_map/all_gather | solution.py:70
Sparse Core Ops, SparseCore 0:
  10.4 37.1 all-gather.5
  1247.4 71.2 reduce-scatter.1
  1320.9 21.2 all-gather.11
Sparse Core Ops, SparseCore 1:
  71.7 227.8 all-gather.9
  492.4 458.4 all-gather.7
  952.4 33.3 all-gather.13
